TPU v7x, 512 devices: a whole 4x8x8 slice. The times are simulated.
512 devices in a mesh: rows: 32 (over y_lo, z, core), cols: 16 (over x, y_hi).
Axes of the slice: x: 4, y: 8 (y_hi: 4, y_lo: 2; y = y_hi * 2 + y_lo), z: 8, core: 2. Of those that a mesh axis runs over, the one named last changes fastest.
Arguments:
- pair_rep: bfloat16 [128, 4096, 128], P('rows', 'cols'), may hold values from -6 to 6
- project_weight: bfloat16 [128, 512], replicated, may hold values from -0.5 to 0.5
- output_weight: bfloat16 [128, 128], replicated, may hold values from -0.5 to 0.5
- pair_bias: bfloat16 [4, 4096, 4096], P(None, 'cols', 'rows'), may hold values from -4 to 300
- chain_valid: int32 [32], replicated, may hold values from 1 to 128, as said below
Outputs:
- update: bfloat16 [128, 4096, 128], P('rows', 'cols')
Inputs may be any that keep to these rules, and one draw needn't show every extreme that they name: Chain c occupies residues c * 128 to (c + 1) * 128 - 1; its first chain_valid[c] residues are valid; some chain is full.
All inputs are finite; a program needn't handle non-finite values.
Results may differ from a plain program's by a relative error of at most 0.0075.
Values may be sent and summed in bfloat16 or wider, within the bound.
No kernel may reach another device: no remote copies, remote signals or barrier semaphores. Data moves between devices by JAX's collectives and lax.ppermute only.
A program may use at most 64 MiB of HBM per device.

v0:
```python
import jax
import jax.numpy as jnp
from jax import lax
from jax.sharding import PartitionSpec as P

SLOT = 128


def attend(carry, query_head, key_piece, value_piece, bias_piece, chain_valid):
    count = key_piece.shape[2]
    position = jnp.arange(count, dtype=jnp.int32)
    chains = chain_valid.shape[0]
    member = (position // SLOT)[:, None] == jnp.arange(chains, dtype=jnp.int32)[None, :]
    allowed = jnp.sum(jnp.where(member, chain_valid[None, :], 0), axis=1)
    mask_add = jnp.where(position % SLOT < allowed, 0.0, -1000000000.0).astype(jnp.float32)
    block = 512

    def step(number, state):
        total, running_max, running_sum = state
        offset = number * block
        key_block = lax.dynamic_slice_in_dim(key_piece, offset, block, 2)
        value_block = lax.dynamic_slice_in_dim(value_piece, offset, block, 2)
        bias_block = lax.dynamic_slice_in_dim(bias_piece, offset, block, 1)
        mask_block = lax.dynamic_slice_in_dim(mask_add, offset, block, 0)
        scores = jnp.einsum(
            "rjd,rdk->rjk", query_head, key_block, preferred_element_type=jnp.float32
        )
        scores = scores + bias_block.astype(jnp.float32)[None] + mask_block[None, None, :]
        new_max = jnp.maximum(running_max, jnp.max(scores, axis=2))
        rescale = jnp.exp(running_max - new_max)
        weights = jnp.exp(scores - new_max[:, :, None])
        running_sum = running_sum * rescale + jnp.sum(weights, axis=2)
        weighted = jnp.einsum(
            "rdk,rjk->rdj",
            value_block,
            weights.astype(jnp.bfloat16),
            preferred_element_type=jnp.float32,
        )
        total = total * rescale[:, None, :] + weighted
        return (total, new_max, running_sum)

    return lax.fori_loop(0, count // block, step, carry)


def local(pair_rep, project_weight, output_weight, pair_bias, chain_valid):
    rows_here, cols_here, width = pair_rep.shape
    heads = pair_bias.shape[0]
    inner = output_weight.shape[0]
    head_size = inner // heads
    pair_f = pair_rep.astype(jnp.float32)
    center = jnp.mean(pair_f, axis=-1, keepdims=True)
    spread = jnp.mean(jnp.square(pair_f - center), axis=-1, keepdims=True)
    normed = ((pair_f - center) * lax.rsqrt(spread + 1e-05)).astype(jnp.bfloat16)
    project = jnp.dot(
        normed.reshape(rows_here * cols_here, width),
        project_weight,
        preferred_element_type=jnp.float32,
    )
    queries = (project[:, :inner] * head_size ** (-0.5)).astype(jnp.bfloat16)
    queries = queries.reshape(rows_here, cols_here, heads, head_size).transpose(0, 2, 1, 3)
    key_part = project[:, inner : 2 * inner].astype(jnp.bfloat16)
    key_part = key_part.reshape(rows_here, cols_here, heads, head_size).transpose(0, 2, 3, 1)
    value_part = project[:, 2 * inner : 3 * inner].astype(jnp.bfloat16)
    value_part = value_part.reshape(rows_here, cols_here, heads, head_size).transpose(0, 2, 3, 1)
    gate = jax.nn.sigmoid(project[:, 3 * inner :])
    outputs = []
    for head_index in range(heads):
        query_head = queries[:, head_index]
        key_head = key_part[:, head_index]
        value_head = value_part[:, head_index]
        bias_head = pair_bias[head_index]
        start_state = (
            jnp.zeros((rows_here, head_size, cols_here), jnp.float32),
            jnp.full((rows_here, cols_here), -jnp.inf, jnp.float32),
            jnp.zeros((rows_here, cols_here), jnp.float32),
        )
        bias_row = lax.all_gather(bias_head, "rows", axis=1, tiled=True)
        state = attend(
            start_state,
            query_head,
            lax.all_gather(key_head, "cols", axis=2, tiled=True),
            lax.all_gather(value_head, "cols", axis=2, tiled=True),
            bias_row,
            chain_valid,
        )
        total, running_max, running_sum = state
        outputs.append(total / running_sum[:, None, :])
    stacked = jnp.stack(outputs, axis=1).transpose(0, 3, 1, 2).reshape(rows_here * cols_here, inner)
    gated = (stacked * gate).astype(jnp.bfloat16)
    update = jnp.dot(gated, output_weight, preferred_element_type=jnp.float32).astype(jnp.bfloat16)
    return update.reshape(rows_here, cols_here, width)


def solution(mesh):
    return jax.shard_map(
        local,
        mesh=mesh,
        in_specs=(P("rows", "cols", None), P(), P(), P(None, "cols", "rows"), P()),
        out_specs=P("rows", "cols", None),
        check_vma=False,
    )
```

profile of v0, /device:TPU:1, one launch (start us, length us, event | category | flops | bytes accessed | tf_op | source)
XLA Modules:
  0.0 814.8 jit_solution(14056148589035336416)
XLA Ops:
  6.5 1.1 convert_reduce_fusion
  7.7 1.3 fusion.34
  9.0 1.3 fusion.35
  21.5 53.6 %all-gather.25.cloned.1.call-done = bf16[4,1,32,4096]{3,0,2,1:T(4,128)(2,1)} async-done(((bf16[4,1,32,256]{3,0,2,1:T(4,128)(2,1)}), bf16[4,1,32,4096]{3,0,2,1:T(4,128)(2,1)}) %all-gather.25.cloned.1.call-update) | async-done | bytes 1048592 | tf_op jit(solution)/shard_map/all_gather | solution.py:81
  75.2 60.8 %all-gather.29.cloned.1.call-done = bf16[4,1,32,4096]{3,0,2,1:T(4,128)(2,1)} async-done(((bf16[4,1,32,256]{3,0,2,1:T(4,128)(2,1)}), bf16[4,1,32,4096]{3,0,2,1:T(4,128)(2,1)}) %all-gather.29.cloned.1.call-update) | async-done | bytes 1048592 | tf_op jit(solution)/shard_map/all_gather | solution.py:82
  135.9 70.5 %all-gather.27.cloned.1.call-done = bf16[1,256,4096]{1,2,0:T(8,128)(2,1)} async-done(((bf16[1,256,128]{1,2,0:T(8,128)(2,1)}), bf16[1,256,4096]{1,2,0:T(8,128)(2,1)}) %all-gather.27.cloned.1.call-update) | async-done | bytes 2097168 | tf_op jit(solution)/shard_map/all_gather | solution.py:77
  206.4 27.7 %while.72 = (s32[]{:T(128)}, f32[4,32,256]{2,1,0:T(8,128)S(1)}, f32[4,256]{1,0:T(4,128)S(1)}, f32[4,256]{1,0:T(4,128)S(1)}, bf16[4,32,4096]{2,0,1:T(4,128)(2,1)}...) while((s32[]{:T(128)}, f32[4,32,256]{2,1,0:T(8,128)S(1)}, ...), condition=%wide.region_6.7_spmd.clone, body=%wide.region_3.6_spmd.clone.sunk | while | flops 71013376 | bytes 8788163 | solution.py:42
  209.9 1.1 constant_dynamic-slice_fusion.12
  213.3 1.1 constant_dynamic-slice_fusion.12
  216.8 1.1 constant_dynamic-slice_fusion.12
  220.3 1.1 constant_dynamic-slice_fusion.12
  223.7 1.1 constant_dynamic-slice_fusion.12
  227.2 1.1 constant_dynamic-slice_fusion.12
  234.1 31.4 %all-gather.35.cloned.1.call-done = bf16[4,1,32,4096]{3,0,2,1:T(4,128)(2,1)} async-done(((bf16[4,1,32,256]{3,0,2,1:T(4,128)(2,1)}), bf16[4,1,32,4096]{3,0,2,1:T(4,128)(2,1)}) %all-gather.35.cloned.1.call-update) | async-done | bytes 1048592 | tf_op jit(solution)/shard_map/all_gather | solution.py:82
  265.6 60.6 %all-gather.31.cloned.1.call-done = bf16[4,1,32,4096]{3,0,2,1:T(4,128)(2,1)} async-done(((bf16[4,1,32,256]{3,0,2,1:T(4,128)(2,1)}), bf16[4,1,32,4096]{3,0,2,1:T(4,128)(2,1)}) %all-gather.31.cloned.1.call-update) | async-done | bytes 1048592 | tf_op jit(solution)/shard_map/all_gather | solution.py:81
  326.2 70.3 %all-gather.33.cloned.1.call-done = bf16[1,256,4096]{1,2,0:T(8,128)(2,1)} async-done(((bf16[1,256,128]{1,2,0:T(8,128)(2,1)}), bf16[1,256,4096]{1,2,0:T(8,128)(2,1)}) %all-gather.33.cloned.1.call-update) | async-done | bytes 2097168 | tf_op jit(solution)/shard_map/all_gather | solution.py:77
  396.5 27.7 %while.73 = (s32[]{:T(128)}, f32[4,32,256]{2,1,0:T(8,128)S(1)}, f32[4,256]{1,0:T(4,128)S(1)}, f32[4,256]{1,0:T(4,128)S(1)}, bf16[4,32,4096]{2,0,1:T(4,128)(2,1)}...) while((s32[]{:T(128)}, f32[4,32,256]{2,1,0:T(8,128)S(1)}, ...), condition=%wide.region_10.11_spmd.clone, body=%wide.region_7.10_spmd.clone.sunk | while | flops 71013376 | bytes 8788163 | solution.py:42
  413.9 1.1 constant_dynamic-slice_fusion.13
  424.2 31.6 %all-gather.37.cloned.1.call-done = bf16[4,1,32,4096]{3,0,2,1:T(4,128)(2,1)} async-done(((bf16[4,1,32,256]{3,0,2,1:T(4,128)(2,1)}), bf16[4,1,32,4096]{3,0,2,1:T(4,128)(2,1)}) %all-gather.37.cloned.1.call-update) | async-done | bytes 1048592 | tf_op jit(solution)/shard_map/all_gather | solution.py:81
  455.9 60.8 %all-gather.41.cloned.1.call-done = bf16[4,1,32,4096]{3,0,2,1:T(4,128)(2,1)} async-done(((bf16[4,1,32,256]{3,0,2,1:T(4,128)(2,1)}), bf16[4,1,32,4096]{3,0,2,1:T(4,128)(2,1)}) %all-gather.41.cloned.1.call-update) | async-done | bytes 1048592 | tf_op jit(solution)/shard_map/all_gather | solution.py:82
  516.7 70.5 %all-gather.39.cloned.1.call-done = bf16[1,256,4096]{1,2,0:T(8,128)(2,1)} async-done(((bf16[1,256,128]{1,2,0:T(8,128)(2,1)}), bf16[1,256,4096]{1,2,0:T(8,128)(2,1)}) %all-gather.39.cloned.1.call-update) | async-done | bytes 2097168 | tf_op jit(solution)/shard_map/all_gather | solution.py:77
  587.1 27.7 %while.74 = (s32[]{:T(128)}, f32[4,32,256]{2,1,0:T(8,128)S(1)}, f32[4,256]{1,0:T(4,128)S(1)}, f32[4,256]{1,0:T(4,128)S(1)}, bf16[4,32,4096]{2,0,1:T(4,128)(2,1)}...) while((s32[]{:T(128)}, f32[4,32,256]{2,1,0:T(8,128)S(1)}, ...), condition=%wide.region_14.15_spmd.clone, body=%wide.region_11.14_spmd.clone.sunk | while | flops 71013376 | bytes 8788163 | solution.py:42
  604.4 1.1 constant_dynamic-slice_fusion.14
  607.9 1.1 constant_dynamic-slice_fusion.14
  611.4 1.1 constant_dynamic-slice_fusion.14
  614.8 31.5 %all-gather.43.cloned.1.call-done = bf16[4,1,32,4096]{3,0,2,1:T(4,128)(2,1)} async-done(((bf16[4,1,32,256]{3,0,2,1:T(4,128)(2,1)}), bf16[4,1,32,4096]{3,0,2,1:T(4,128)(2,1)}) %all-gather.43.cloned.1.call-update) | async-done | bytes 1048592 | tf_op jit(solution)/shard_map/all_gather | solution.py:81
  646.3 60.8 %all-gather.47.cloned.1.call-done = bf16[4,1,32,4096]{3,0,2,1:T(4,128)(2,1)} async-done(((bf16[4,1,32,256]{3,0,2,1:T(4,128)(2,1)}), bf16[4,1,32,4096]{3,0,2,1:T(4,128)(2,1)}) %all-gather.47.cloned.1.call-update) | async-done | bytes 1048592 | tf_op jit(solution)/shard_map/all_gather | solution.py:82
  707.1 70.3 %all-gather.45.cloned.1.call-done = bf16[1,256,4096]{1,2,0:T(8,128)(2,1)} async-done(((bf16[1,256,128]{1,2,0:T(8,128)(2,1)}), bf16[1,256,4096]{1,2,0:T(8,128)(2,1)}) %all-gather.45.cloned.1.call-update) | async-done | bytes 2097168 | tf_op jit(solution)/shard_map/all_gather | solution.py:77
  777.4 27.7 %while.75 = (s32[]{:T(128)}, f32[4,32,256]{2,1,0:T(8,128)S(1)}, f32[4,256]{1,0:T(4,128)S(1)}, f32[4,256]{1,0:T(4,128)S(1)}, bf16[4,32,4096]{2,0,1:T(4,128)(2,1)}...) while((s32[]{:T(128)}, f32[4,32,256]{2,1,0:T(8,128)S(1)}, ...), condition=%wide.region_18.19_spmd.clone, body=%wide.region_15.18_spmd.clone.sunk | while | flops 71013376 | bytes 8788163 | solution.py:42
  784.4 1.1 constant_dynamic-slice_fusion.15
  798.2 1.1 constant_dynamic-slice_fusion.15
  806.0 2.0 convolution_convert_fusion
  (354 shorter events, 107.6 us)
Async XLA Ops:
  6.5 3.8 copy-start
  6.5 68.6 %all-gather.25.cloned.1.call-start = ((), (), s32[]{:S(2)}) async-start(), calls=%async_computation | async-start | bytes 1114112 | tf_op jit(solution)/shard_map/all_gather | solution.py:81
  10.8 10.0 %copy-start.1 = (f32[1024,512]{1,0:T(8,128)}, f32[1024,512]{1,0:T(8,128)S(1)}, u32[]{:S(2)}) copy-start(f32[1024,512]{1,0:T(8,128)S(1)} %get-tuple-element.940) | copy-start | bytes 6291460
  10.8 2.6 copy-start.2
  12.1 123.8 %all-gather.29.cloned.1.call-start = ((), (), s32[]{:S(2)}) async-start(), calls=%async_computation.2 | async-start | bytes 1114112 | tf_op jit(solution)/shard_map/all_gather | solution.py:82
  13.3 8.0 copy-start.3
  13.3 193.1 %all-gather.27.cloned.1.call-start = ((), (), s32[]{:S(2)}) async-start(), calls=%async_computation.1 | async-start | bytes 2162688 | tf_op jit(solution)/shard_map/all_gather | solution.py:77
  14.2 251.4 %all-gather.35.cloned.1.call-start = ((), (), s32[]{:S(2)}) async-start(), calls=%async_computation.5 | async-start | bytes 1114112 | tf_op jit(solution)/shard_map/all_gather | solution.py:82
  14.8 311.4 %all-gather.31.cloned.1.call-start = ((), (), s32[]{:S(2)}) async-start(), calls=%async_computation.3 | async-start | bytes 1114112 | tf_op jit(solution)/shard_map/all_gather | solution.py:81
  15.4 381.2 %all-gather.33.cloned.1.call-start = ((), (), s32[]{:S(2)}) async-start(), calls=%async_computation.4 | async-start | bytes 2162688 | tf_op jit(solution)/shard_map/all_gather | solution.py:77
  16.2 439.7 %all-gather.37.cloned.1.call-start = ((), (), s32[]{:S(2)}) async-start(), calls=%async_computation.6 | async-start | bytes 1114112 | tf_op jit(solution)/shard_map/all_gather | solution.py:81
  16.9 499.7 %all-gather.41.cloned.1.call-start = ((), (), s32[]{:S(2)}) async-start(), calls=%async_computation.8 | async-start | bytes 1114112 | tf_op jit(solution)/shard_map/all_gather | solution.py:82
  17.7 569.5 %all-gather.39.cloned.1.call-start = ((), (), s32[]{:S(2)}) async-start(), calls=%async_computation.7 | async-start | bytes 2162688 | tf_op jit(solution)/shard_map/all_gather | solution.py:77
  18.5 627.8 %all-gather.43.cloned.1.call-start = ((), (), s32[]{:S(2)}) async-start(), calls=%async_computation.9 | async-start | bytes 1114112 | tf_op jit(solution)/shard_map/all_gather | solution.py:81
  19.1 688.0 %all-gather.47.cloned.1.call-start = ((), (), s32[]{:S(2)}) async-start(), calls=%async_computation.11 | async-start | bytes 1114112 | tf_op jit(solution)/shard_map/all_gather | solution.py:82
  19.8 757.6 %all-gather.45.cloned.1.call-start = ((), (), s32[]{:S(2)}) async-start(), calls=%async_computation.10 | async-start | bytes 2162688 | tf_op jit(solution)/shard_map/all_gather | solution.py:77
  805.2 0.8 copy-start.4
Sparse Core Ops, SparseCore 0:
  12.3 62.8 all-gather.24
  78.1 57.7 all-gather.28
  138.1 68.2 all-gather.26
  209.3 56.2 all-gather.34
  268.4 57.7 all-gather.30
  328.2 68.2 all-gather.32
  399.5 56.3 all-gather.36
  458.9 57.7 all-gather.40
  518.8 68.2 all-gather.38
  590.0 56.2 all-gather.42
  649.3 57.7 all-gather.46
  709.1 68.2 all-gather.44
where the time goes:
time: 817 us; the launch traced here: 815 us
  waiting for transfers between devices  677 us (83%)
  other arithmetic  46.2 us (6%)
  local copies, waits for them, and re-layouts  43.4 us (5%)
  matrix products  32.4 us (4%)
  between operations  13.9 us (2%)
    all_gather x4, waiting for transfers between devices, local(): bias_row = lax.all_gather(bias_head, 'rows', axis=1, tiled=True)  282 us
    all_gather x4, waiting for transfers between devices, local(): lax.all_gather(value_head, 'cols', axis=2, tiled=True)  214 us
    all_gather x4, waiting for transfers between devices, local(): lax.all_gather(key_head, 'cols', axis=2, tiled=True)  177 us
    dynamic_slice x32, local copies, waits for them, and re-layouts, step(): value_block = lax.dynamic_slice_in_dim(value_piece, offset, block, 2)  34.1 us
    convert_element_type x32, other arithmetic, step(): bias_block.astype(jnp.float32)[None]  31.8 us
    dot_general x32, matrix products, step(): jnp.einsum('rjd,rdk->rjk', query_head, key_block, preferred_element_type=...  16.6 us
  transfers between devices with their start and end apart: 12, of which 12 were waited for; matrix products, arithmetic and copies ran while one was open for 11% of the time, Pallas kernels for 0%

commit v1 on v0

--- a/solution.py
+++ b/solution.py
@@ -74,7 +74,16 @@
             jnp.full((rows_here, cols_here), -jnp.inf, jnp.float32),
             jnp.zeros((rows_here, cols_here), jnp.float32),
         )
-        bias_row = lax.all_gather(bias_head, "rows", axis=1, tiled=True)
+
+        def _update_slots(device_axis, z):
+            return jnp.concatenate(
+                lax.all_to_all(
+                    jnp.stack([z for _ in range(lax.psum(1, device_axis))]), device_axis, 0, 0
+                ),
+                axis=1,
+            )
+
+        bias_row = _update_slots("rows", bias_head)
         state = attend(
             start_state,
             query_head,

time: 817 us -> 552 us (0.68)
  waiting for transfers between devices: 677 us -> 368 us
  starting transfers between devices: 0.44 us -> 39.6 us
    all_gather x4 -> x0, waiting for transfers between devices: 282 us -> none  [local(): bias_row = lax.all_gather(bias_head, 'rows', axis=1, tiled=True)]
    all_gather x4, waiting for transfers between devices: 177 us -> 84.1 us  [local(): lax.all_gather(key_head, 'cols', axis=2, tiled=True)]
    all_to_all x0 -> x4, waiting for transfers between devices: none -> 49.5 us  [_update_slots(): lax.all_to_all(jnp.stack([z for _ in range(lax.psum(1, device_axis))]), d...]
    all_to_all x0 -> x4, starting transfers between devices: none -> 39.3 us  [_update_slots(): lax.all_to_all(jnp.stack([z for _ in range(lax.psum(1, device_axis))]), d...]
    all_gather x4, waiting for transfers between devices: 214 us -> 231 us  [local(): lax.all_gather(value_head, 'cols', axis=2, tiled=True)]
  transfers between devices with their start and end apart: 12 -> 12, of which waited for: 12 -> 8; matrix products, arithmetic and copies ran while one was open for 11% -> 16% of each run, Pallas kernels for 0% -> 0%
where the time goes in v1:
time: 552 us; the launch traced here: 550 us
  waiting for transfers between devices  368 us (67%)
  local copies, waits for them, and re-layouts  47.4 us (9%)
  other arithmetic  46.2 us (8%)
  starting transfers between devices  39.6 us (7%)
  matrix products  32.5 us (6%)
  between operations  14 us (3%)
    all_gather x4, waiting for transfers between devices, local(): lax.all_gather(value_head, 'cols', axis=2, tiled=True)  231 us
    all_gather x4, waiting for transfers between devices, local(): lax.all_gather(key_head, 'cols', axis=2, tiled=True)  84.1 us
    all_to_all x4, waiting for transfers between devices, _update_slots(): lax.all_to_all(jnp.stack([z for _ in range(lax.psum(1, device_axis))]), d...  49.5 us
    all_to_all x4, starting transfers between devices, _update_slots(): lax.all_to_all(jnp.stack([z for _ in range(lax.psum(1, device_axis))]), d...  39.3 us
    dynamic_slice x32, local copies, waits for them, and re-layouts, step(): value_block = lax.dynamic_slice_in_dim(value_piece, offset, block, 2)  34.1 us
    convert_element_type x32, other arithmetic, step(): bias_block.astype(jnp.float32)[None]  31.8 us
    dot_general x32, matrix products, step(): jnp.einsum('rjd,rdk->rjk', query_head, key_block, preferred_element_type=...  16.7 us
    dot_general x32, matrix products, step(): jnp.einsum('rdk,rjk->rdj', value_block, weights.astype(jnp.bfloat16), pre...  13.4 us
  transfers between devices with their start and end apart: 12, of which 8 were waited for; matrix products, arithmetic and copies ran while one was open for 16% of the time, Pallas kernels for 0%

profile of v1, /device:TPU:1, one launch (start us, length us, event | category | flops | bytes accessed | tf_op | source)
XLA Modules:
  0.0 549.6 jit_solution(4339789104742517282)
XLA Ops:
  6.5 1.1 convert_reduce_fusion
  7.7 1.3 fusion.34
  9.0 1.3 fusion.35
  16.0 1.6 stack.27
  17.6 13.0 %all-to-all-start = ((bf16[32,256,128]{1,2,0:T(8,128)(2,1)}), bf16[32,256,128]{1,2,0:T(8,128)(2,1)}, u32[]{:S(2)}, u32[]{:S(2)}) async-start(bf16[32,256,128]{1,2,0:T(8,128)(2,1)} %stack.27), calls=%async_computation | async-start | bytes 4194304 | tf_op jit(solution)/shard_map/all_to_all | solution.py:80
  33.4 49.5 %all-to-all-done = bf16[32,256,128]{1,2,0:T(8,128)(2,1)} async-done(((bf16[32,256,128]{1,2,0:T(8,128)(2,1)}), bf16[32,256,128]{1,2,0:T(8,128)(2,1)}, u32[]{:S(2)}, u32[]{:S(2)}) %all-to-all-start) | async-done | bytes 2097184 | tf_op jit(solution)/shard_map/all_to_all | solution.py:80
  82.9 1.6 stack.29
  84.6 5.5 %all-to-all-start.1 = ((bf16[32,256,128]{1,2,0:T(8,128)(2,1)}), bf16[32,256,128]{1,2,0:T(8,128)(2,1)}, u32[]{:S(2)}, u32[]{:S(2)}) async-start(bf16[32,256,128]{1,2,0:T(8,128)(2,1)} %stack.29), calls=%async_computation.1 | async-start | bytes 4194304 | tf_op jit(solution)/shard_map/all_to_all | solution.py:80
  90.2 49.7 %all-gather.19.cloned.1.call-done = bf16[4,1,32,4096]{3,0,2,1:T(4,128)(2,1)} async-done(((bf16[4,1,32,256]{3,0,2,1:T(4,128)(2,1)}), bf16[4,1,32,4096]{3,0,2,1:T(4,128)(2,1)}) %all-gather.19.cloned.1.call-update) | async-done | bytes 1048592 | tf_op jit(solution)/shard_map/all_gather | solution.py:91
  139.9 27.7 %while.72 = (s32[]{:T(128)}, f32[4,32,256]{2,1,0:T(8,128)S(1)}, f32[4,256]{1,0:T(4,128)S(1)}, f32[4,256]{1,0:T(4,128)S(1)}, bf16[4,32,4096]{2,0,1:T(4,128)(2,1)}...) while((s32[]{:T(128)}, f32[4,32,256]{2,1,0:T(8,128)S(1)}, ...), condition=%wide.region_6.7_spmd.clone, body=%wide.region_3.6_spmd.clone.sunk | while | flops 71013376 | bytes 8788163 | solution.py:42
  143.3 1.1 constant_dynamic-slice_fusion.12
  153.7 1.1 constant_dynamic-slice_fusion.12
  157.2 1.1 constant_dynamic-slice_fusion.12
  167.6 1.6 stack.31
  169.3 10.3 %all-to-all-start.2 = ((bf16[32,256,128]{1,2,0:T(8,128)(2,1)}), bf16[32,256,128]{1,2,0:T(8,128)(2,1)}, u32[]{:S(2)}, u32[]{:S(2)}) async-start(bf16[32,256,128]{1,2,0:T(8,128)(2,1)} %stack.31), calls=%async_computation.2 | async-start | bytes 4194304 | tf_op jit(solution)/shard_map/all_to_all | solution.py:80
  179.6 25.6 %all-gather.21.cloned.1.call-done = bf16[4,1,32,4096]{3,0,2,1:T(4,128)(2,1)} async-done(((bf16[4,1,32,256]{3,0,2,1:T(4,128)(2,1)}), bf16[4,1,32,4096]{3,0,2,1:T(4,128)(2,1)}) %all-gather.21.cloned.1.call-update) | async-done | bytes 1048592 | tf_op jit(solution)/shard_map/all_gather | solution.py:90
  205.2 60.2 %all-gather.23.cloned.1.call-done = bf16[4,1,32,4096]{3,0,2,1:T(4,128)(2,1)} async-done(((bf16[4,1,32,256]{3,0,2,1:T(4,128)(2,1)}), bf16[4,1,32,4096]{3,0,2,1:T(4,128)(2,1)}) %all-gather.23.cloned.1.call-update) | async-done | bytes 1048592 | tf_op jit(solution)/shard_map/all_gather | solution.py:91
  265.4 27.7 %while.73 = (s32[]{:T(128)}, f32[4,32,256]{2,1,0:T(8,128)S(1)}, f32[4,256]{1,0:T(4,128)S(1)}, f32[4,256]{1,0:T(4,128)S(1)}, bf16[4,32,4096]{2,0,1:T(4,128)(2,1)}...) while((s32[]{:T(128)}, f32[4,32,256]{2,1,0:T(8,128)S(1)}, ...), condition=%wide.region_10.11_spmd.clone, body=%wide.region_7.10_spmd.clone.sunk | while | flops 71013376 | bytes 8788163 | solution.py:42
  272.3 1.1 constant_dynamic-slice_fusion.13
  282.7 1.1 constant_dynamic-slice_fusion.13
  293.1 1.6 stack.33
  294.7 10.4 %all-to-all-start.3 = ((bf16[32,256,128]{1,2,0:T(8,128)(2,1)}), bf16[32,256,128]{1,2,0:T(8,128)(2,1)}, u32[]{:S(2)}, u32[]{:S(2)}) async-start(bf16[32,256,128]{1,2,0:T(8,128)(2,1)} %stack.33), calls=%async_computation.3 | async-start | bytes 4194304 | tf_op jit(solution)/shard_map/all_to_all | solution.py:80
  305.1 25.5 %all-gather.25.cloned.1.call-done = bf16[4,1,32,4096]{3,0,2,1:T(4,128)(2,1)} async-done(((bf16[4,1,32,256]{3,0,2,1:T(4,128)(2,1)}), bf16[4,1,32,4096]{3,0,2,1:T(4,128)(2,1)}) %all-gather.25.cloned.1.call-update) | async-done | bytes 1048592 | tf_op jit(solution)/shard_map/all_gather | solution.py:90
  330.6 60.2 %all-gather.27.cloned.1.call-done = bf16[4,1,32,4096]{3,0,2,1:T(4,128)(2,1)} async-done(((bf16[4,1,32,256]{3,0,2,1:T(4,128)(2,1)}), bf16[4,1,32,4096]{3,0,2,1:T(4,128)(2,1)}) %all-gather.27.cloned.1.call-update) | async-done | bytes 1048592 | tf_op jit(solution)/shard_map/all_gather | solution.py:91
  390.8 27.7 %while.74 = (s32[]{:T(128)}, f32[4,32,256]{2,1,0:T(8,128)S(1)}, f32[4,256]{1,0:T(4,128)S(1)}, f32[4,256]{1,0:T(4,128)S(1)}, bf16[4,32,4096]{2,0,1:T(4,128)(2,1)}...) while((s32[]{:T(128)}, f32[4,32,256]{2,1,0:T(8,128)S(1)}, ...), condition=%wide.region_14.15_spmd.clone, body=%wide.region_11.14_spmd.clone.sunk | while | flops 71013376 | bytes 8788163 | solution.py:42
  408.1 1.1 constant_dynamic-slice_fusion.14
  418.5 33.0 %all-gather.29.cloned.1.call-done = bf16[4,1,32,4096]{3,0,2,1:T(4,128)(2,1)} async-done(((bf16[4,1,32,256]{3,0,2,1:T(4,128)(2,1)}), bf16[4,1,32,4096]{3,0,2,1:T(4,128)(2,1)}) %all-gather.29.cloned.1.call-update) | async-done | bytes 1048592 | tf_op jit(solution)/shard_map/all_gather | solution.py:90
  451.5 60.8 %all-gather.31.cloned.1.call-done = bf16[4,1,32,4096]{3,0,2,1:T(4,128)(2,1)} async-done(((bf16[4,1,32,256]{3,0,2,1:T(4,128)(2,1)}), bf16[4,1,32,4096]{3,0,2,1:T(4,128)(2,1)}) %all-gather.31.cloned.1.call-update) | async-done | bytes 1048592 | tf_op jit(solution)/shard_map/all_gather | solution.py:91
  512.3 27.7 %while.75 = (s32[]{:T(128)}, f32[4,32,256]{2,1,0:T(8,128)S(1)}, f32[4,256]{1,0:T(4,128)S(1)}, f32[4,256]{1,0:T(4,128)S(1)}, bf16[4,32,4096]{2,0,1:T(4,128)(2,1)}...) while((s32[]{:T(128)}, f32[4,32,256]{2,1,0:T(8,128)S(1)}, ...), condition=%wide.region_18.19_spmd.clone, body=%wide.region_15.18_spmd.clone.sunk | while | flops 71013376 | bytes 8788163 | solution.py:42
  515.7 1.1 constant_dynamic-slice_fusion.15
  519.2 1.1 constant_dynamic-slice_fusion.15
  540.8 2.0 convolution_convert_fusion
  (354 shorter events, 109.2 us)
Async XLA Ops:
  6.5 3.8 copy-start
  6.5 83.6 %all-gather.17.cloned.1.call-start = ((), (), s32[]{:S(2)}) async-start(), calls=%async_computation.4 | async-start | bytes 1114112 | tf_op jit(solution)/shard_map/all_gather | solution.py:90
  10.7 21.5 %copy-start.1 = (f32[1024,512]{1,0:T(8,128)}, f32[1024,512]{1,0:T(8,128)S(1)}, u32[]{:S(2)}) copy-start(f32[1024,512]{1,0:T(8,128)S(1)} %get-tuple-element.940) | copy-start | bytes 6291460
  10.8 5.1 copy-start.2
  12.1 127.7 %all-gather.19.cloned.1.call-start = ((), (), s32[]{:S(2)}) async-start(), calls=%async_computation.5 | async-start | bytes 1114112 | tf_op jit(solution)/shard_map/all_gather | solution.py:91
  13.4 191.8 %all-gather.21.cloned.1.call-start = ((), (), s32[]{:S(2)}) async-start(), calls=%async_computation.6 | async-start | bytes 1114112 | tf_op jit(solution)/shard_map/all_gather | solution.py:90
  14.1 251.3 %all-gather.23.cloned.1.call-start = ((), (), s32[]{:S(2)}) async-start(), calls=%async_computation.7 | async-start | bytes 1114112 | tf_op jit(solution)/shard_map/all_gather | solution.py:91
  14.7 315.9 %all-gather.25.cloned.1.call-start = ((), (), s32[]{:S(2)}) async-start(), calls=%async_computation.8 | async-start | bytes 1114112 | tf_op jit(solution)/shard_map/all_gather | solution.py:90
  15.3 375.5 %all-gather.27.cloned.1.call-start = ((), (), s32[]{:S(2)}) async-start(), calls=%async_computation.9 | async-start | bytes 1114112 | tf_op jit(solution)/shard_map/all_gather | solution.py:91
  17.6 65.3 %all-to-all-start = ((bf16[32,256,128]{1,2,0:T(8,128)(2,1)}), bf16[32,256,128]{1,2,0:T(8,128)(2,1)}, u32[]{:S(2)}, u32[]{:S(2)}) async-start(bf16[32,256,128]{1,2,0:T(8,128)(2,1)} %stack.27), calls=%async_computation | async-start | bytes 4194304 | tf_op jit(solution)/shard_map/all_to_all | solution.py:80
  30.6 2.6 copy-start.3
  30.6 420.8 %all-gather.29.cloned.1.call-start = ((), (), s32[]{:S(2)}) async-start(), calls=%async_computation.10 | async-start | bytes 1114112 | tf_op jit(solution)/shard_map/all_gather | solution.py:90
  31.4 480.9 %all-gather.31.cloned.1.call-start = ((), (), s32[]{:S(2)}) async-start(), calls=%async_computation.11 | async-start | bytes 1114112 | tf_op jit(solution)/shard_map/all_gather | solution.py:91
  84.6 83.0 %all-to-all-start.1 = ((bf16[32,256,128]{1,2,0:T(8,128)(2,1)}), bf16[32,256,128]{1,2,0:T(8,128)(2,1)}, u32[]{:S(2)}, u32[]{:S(2)}) async-start(bf16[32,256,128]{1,2,0:T(8,128)(2,1)} %stack.29), calls=%async_computation.1 | async-start | bytes 4194304 | tf_op jit(solution)/shard_map/all_to_all | solution.py:80
  169.3 123.8 %all-to-all-start.2 = ((bf16[32,256,128]{1,2,0:T(8,128)(2,1)}), bf16[32,256,128]{1,2,0:T(8,128)(2,1)}, u32[]{:S(2)}, u32[]{:S(2)}) async-start(bf16[32,256,128]{1,2,0:T(8,128)(2,1)} %stack.31), calls=%async_computation.2 | async-start | bytes 4194304 | tf_op jit(solution)/shard_map/all_to_all | solution.py:80
  294.7 217.5 %all-to-all-start.3 = ((bf16[32,256,128]{1,2,0:T(8,128)(2,1)}), bf16[32,256,128]{1,2,0:T(8,128)(2,1)}, u32[]{:S(2)}, u32[]{:S(2)}) async-start(bf16[32,256,128]{1,2,0:T(8,128)(2,1)} %stack.33), calls=%async_computation.3 | async-start | bytes 4194304 | tf_op jit(solution)/shard_map/all_to_all | solution.py:80
  540.0 0.8 copy-start.4
Sparse Core Ops, SparseCore 0:
  12.3 65.4 all-gather.16
  80.8 59.0 all-gather.18
  142.9 62.2 all-gather.20
  208.0 57.2 all-gather.22
  268.2 62.3 all-gather.24
  333.5 57.2 all-gather.26
  393.7 57.6 all-gather.28
  454.5 57.7 all-gather.30
